TPU v7x, 32 devices: a whole 2x2x4 slice. The times are simulated.
32 devices in a mesh: blk: 8 (over y, x, core), grp: 4 (over z).
Axes of the slice: x: 2, y: 2, z: 4, core: 2. Of those that a mesh axis runs over, the one named last changes fastest.
Arguments:
- currents: bfloat16 [4, 16, 65536], P('grp', None, 'blk'), may hold values from -6 to 6
- background: float32 [4, 16, 65536], P('grp', None, 'blk'), may hold values from -6 to 6
- green: bfloat16 [4, 512, 8, 128, 128], P('grp', 'blk'), may hold values from -0.1875 to 0.1875
- offsets: int32 [4, 512, 8], P('grp', 'blk'), may hold values from -128 to 128
- station_cells: int32 [2048, 4], P(('blk', 'grp')), may hold values from 0 to 2047, as said below
- station_green: bfloat16 [2048, 4, 128], P(('blk', 'grp')), may hold values from -0.25 to 0.25
- station_background: float32 [16, 2048], P(None, ('blk', 'grp')), may hold values from -6 to 6
Outputs:
- cell_field: float32 [4, 16, 65536], P('grp', None, 'blk')
- station_field: float32 [16, 2048], P(None, ('blk', 'grp'))
Inputs may be any that keep to these rules, and one draw needn't show every extreme that they name: `station_cells`: station s lies with device flat index s // 64; its near blocks lie in blocks from (s // 256 - 1) * 64 to (s // 256 + 2) * 64 - 1, taken modulo 512, in any slab.
All inputs are finite; a program needn't handle non-finite values.
Results may differ from a plain program's by a relative error of at most 0.0003.
Values may be sent and summed in bfloat16 or wider, within the bound.
A program may use at most 64 MiB of HBM per device.

v0:
```python
import jax
import jax.numpy as jnp
from jax import lax
from jax.sharding import PartitionSpec as P

REACH = 2


def from_behind(array, axis, by):
    peers = lax.axis_size(axis)
    return lax.ppermute(array, axis, [(i, (i + by) % peers) for i in range(peers)])


def body(currents, background, green, offsets, station_cells, station_green, station_background):
    local = currents[0]
    n_cols = local.shape[0]
    blocks = green.shape[1]
    cells = green.shape[3]
    span = blocks * cells
    here = lax.axis_index("blk")
    slab_blocks = blocks * lax.axis_size("blk")
    upper = []
    lower = []
    moving = local
    for step in range(REACH):
        moving = from_behind(moving, "blk", -1)
        upper.append(moving)
    moving = local
    for step in range(REACH):
        moving = from_behind(moving, "blk", 1)
        lower.append(moving)
    window = jnp.concatenate(lower[::-1] + [local] + upper, axis=1)
    window_blocks = window.reshape(n_cols, (2 * REACH + 1) * blocks, cells)
    source = jnp.arange(blocks, dtype=jnp.int32)[:, None] + offsets[0] + REACH * blocks
    picked = window_blocks[:, source, :]
    anomalous = jnp.einsum("bkpq,cbkq->cbp", green[0], picked, preferred_element_type=jnp.float32)
    cell_field = background + anomalous.reshape(1, n_cols, span)
    slab_stack = lax.all_gather(currents, "grp", axis=0, tiled=True)
    below = from_behind(slab_stack, "blk", 1)
    above = from_behind(slab_stack, "blk", -1)
    near = jnp.concatenate([below, slab_stack, above], axis=2)
    n_slabs = near.shape[0]
    near_blocks = near.reshape(n_slabs, n_cols, 3 * blocks, cells)
    slab_index = station_cells // slab_blocks
    position = (station_cells % slab_blocks - (here - 1) * blocks) % slab_blocks
    chosen = near_blocks[slab_index, :, position, :]
    station_field = station_background + jnp.einsum(
        "skp,skcp->cs", station_green, chosen, preferred_element_type=jnp.float32
    )
    return (cell_field, station_field)


def solution(mesh):
    return jax.shard_map(
        body,
        mesh=mesh,
        in_specs=(
            P("grp", None, "blk"),
            P("grp", None, "blk"),
            P("grp", "blk", None, None, None),
            P("grp", "blk", None),
            P(("blk", "grp"), None),
            P(("blk", "grp"), None, None),
            P(None, ("blk", "grp")),
        ),
        out_specs=(P("grp", None, "blk"), P(None, ("blk", "grp"))),
        check_vma=False,
    )
```

profile of v0, /device:TPU:1, one launch (start us, length us, event | category | flops | bytes accessed | tf_op | source)
XLA Modules:
  0.0 79.5 jit_solution(7111683563668175119)
XLA Ops:
  7.2 0.7 all-gather.2.cloned.1.call-update
  7.9 2.7 %collective-permute-start = (bf16[16,8192]{1,0:T(8,128)(2,1)}, bf16[16,8192]{1,0:T(8,128)(2,1)S(1)}, u32[]{:S(2)}, u32[]{:S(2)}) collective-permute-start(bf16[16,8192]{1,0:T(8,128)(2,1)} %bitcast.59), channel_id=1, source_target_pairs={{0,4},{4,8},{8,12},{12,16},{16,20},{20,24},{24,28},{28,0},{1,5},{5... | collective-permute-start | bytes 786440 | tf_op jit(solution)/shard_map/ppermute | solution.py:11
  10.6 1.0 %copy.39 = bf16[2,8,64,128]{3,2,1,0:T(8,128)(2,1)S(1)} copy(bf16[2,8,64,128]{3,1,2,0:T(8,128)(2,1)} %bitcast.61) | data formatting | bytes 524288
  11.6 0.7 compare_select_fusion
  12.5 3.5 %collective-permute-done = bf16[16,8192]{1,0:T(8,128)(2,1)S(1)} collective-permute-done((bf16[16,8192]{1,0:T(8,128)(2,1)}, bf16[16,8192]{1,0:T(8,128)(2,1)S(1)}, u32[]{:S(2)}, u32[]{:S(2)}) %collective-permute-start) | collective-permute-done | bytes 262176 | tf_op jit(solution)/shard_map/ppermute | solution.py:11
  16.0 2.4 %collective-permute-start.1 = (bf16[16,8192]{1,0:T(8,128)(2,1)S(1)}, bf16[16,8192]{1,0:T(8,128)(2,1)S(1)}, u32[]{:S(2)}, u32[]{:S(2)}) collective-permute-start(bf16[16,8192]{1,0:T(8,128)(2,1)S(1)} %collective-permute-done), channel_id=1, source_target_pairs={{0,4},{4,8},{8,12},{12,16},{16,20},{20,24},{24,28},{28,0},{1,5},{5... | collective-permute-start | bytes 786440 | tf_op jit(solution)/shard_map/ppermute | solution.py:11
  18.3 0.7 fusion.11
  19.1 0.1 copy.29
  19.2 0.1 reshape.56
  19.3 3.1 %collective-permute-done.1 = bf16[16,8192]{1,0:T(8,128)(2,1)S(1)} collective-permute-done((bf16[16,8192]{1,0:T(8,128)(2,1)S(1)}, bf16[16,8192]{1,0:T(8,128)(2,1)S(1)}, u32[]{:S(2)}, u32[]{:S(2)}) %collective-permute-start.1) | collective-permute-done | bytes 262176 | tf_op jit(solution)/shard_map/ppermute | solution.py:11
  22.6 0.2 copy_dynamic-update-slice_fusion
  22.9 16.6 %all-gather.2.cloned.1.call-done = bf16[4,16,8192]{2,1,0:T(8,128)(2,1)} async-done(((bf16[1,16,8192]{2,1,0:T(8,128)(2,1)}), bf16[4,16,8192]{2,1,0:T(8,128)(2,1)}) %all-gather.2.cloned.1.call-update) | async-done | bytes 1048592 | tf_op jit(solution)/shard_map/all_gather | solution.py:38
  39.5 1.9 %collective-permute-start.4 = (bf16[4,16,8192]{2,1,0:T(8,128)(2,1)}, bf16[4,16,8192]{2,1,0:T(8,128)(2,1)}, u32[]{:S(2)}, u32[]{:S(2)}) collective-permute-start(bf16[4,16,8192]{2,1,0:T(8,128)(2,1)} %all-gather.2.cloned.1.call-done), channel_id=1, source_target_pairs={{0,4},{4,8},{8,12},{12,16},{16,20},{20,24},{24,28},{28,0},{1,5},{5... | collective-permute-start | bytes 3145736 | tf_op jit(solution)/shard_map/ppermute | solution.py:11
  41.5 2.0 %gather_fusion = bf16[512,16,128]{2,1,0:T(8,128)(2,1)S(1)} fusion(bf16[16,320,128]{2,0,1:T(8,128)(2,1)S(1)} %bitcast_dynamic-update-slice_fusion, s32[1024]{0:T(1024)S(1)} %pad_clamp_fusion), kind=kCustom, calls=%fused_computation | custom fusion | bytes 4196352 | tf_op jit(solution)/shard_map/gather | solution.py:35
  43.5 8.1 %fusion.2 = f32[16,64,128]{2,0,1:T(8,128)S(1)} fusion(bf16[16,64,8,128]{3,0,2,1:T(8,128)(2,1)S(1)} %bitcast.57, bf16[1,64,8,128,128]{4,3,2,1,0:T(8,128)(2,1)} %param.9), kind=kOutput, calls=%fused_computation.6 | convolution fusion | flops 268435456 | bytes 19398656 | tf_op jit(solution)/shard_map/bkpq,cbkq->cbp/dot_general | solution.py:36
  51.6 0.2 copy.28
  51.9 0.8 copy-done.2
  52.6 0.8 %add.79 = f32[1,16,8192]{2,1,0:T(8,128)} add(f32[1,16,8192]{2,1,0:T(8,128)S(1)} %copy-done.2, f32[1,16,8192]{2,1,0:T(8,128)S(1)} %reshape.46) | non-fusion elementwise | flops 131072 | bytes 1572864 | tf_op jit(solution)/shard_map/add | solution.py:37
  53.5 9.4 %collective-permute-done.4 = bf16[4,16,8192]{2,1,0:T(8,128)(2,1)} collective-permute-done((bf16[4,16,8192]{2,1,0:T(8,128)(2,1)}, bf16[4,16,8192]{2,1,0:T(8,128)(2,1)}, u32[]{:S(2)}, u32[]{:S(2)}) %collective-permute-start.4) | collective-permute-done | bytes 1048608 | tf_op jit(solution)/shard_map/ppermute | solution.py:11
  62.9 3.4 %collective-permute-done.5 = bf16[4,16,8192]{2,1,0:T(8,128)(2,1)} collective-permute-done((bf16[4,16,8192]{2,1,0:T(8,128)(2,1)}, bf16[4,16,8192]{2,1,0:T(8,128)(2,1)}, u32[]{:S(2)}, u32[]{:S(2)}) %collective-permute-start.5) | collective-permute-done | bytes 1048608 | tf_op jit(solution)/shard_map/ppermute | solution.py:11
  66.3 1.8 %copy_bitcast_fusion = bf16[4,16,192,128]{3,1,2,0:T(8,128)(2,1)S(1)} fusion(bf16[4,16,8192]{2,1,0:T(8,128)(2,1)} %collective-permute-done.5, bf16[4,16,8192]{2,1,0:T(8,128)(2,1)S(1)} %copy-done.1, bf16[4,16,8192]{2,1,0:T(8,128)(2,1)} %collective-permute-done.4), kind=kLoop, calls=%fused_computation.4 | loop fusion | flops 9437184 | bytes 6291456 | tf_op jit(solution)/shard_map/reshape | solution.py:43
  68.1 2.2 %gather_fusion.1 = bf16[256,16,128]{2,1,0:T(8,128)(2,1)} fusion(bf16[4,16,192,128]{3,1,2,0:T(8,128)(2,1)S(1)} %copy_bitcast_fusion, s32[256]{0:T(256)S(1)} %reshape.56), kind=kCustom, calls=%fused_computation.1 | custom fusion | bytes 2099200 | tf_op jit(solution)/shard_map/gather | solution.py:46
  70.3 1.6 %fusion.5 = f32[64,1,16,1]{2,1,3,0:T(1,128)S(1)} fusion(bf16[64,4,16,128]{3,2,1,0:T(8,128)(2,1)} %bitcast.58, bf16[64,4,128,1]{2,1,0,3:T(4,128)(2,1)S(1)} %bitcast.56), kind=kOutput, calls=%fused_computation.12 | convolution fusion | flops 1048576 | bytes 1118208 | tf_op jit(solution)/shard_map/skp,skcp->cs/dot_general | solution.py:47
  72.0 0.6 bitcast_add_fusion
  (22 shorter events, 0.7 us)
Async XLA Ops:
  7.2 63.2 %copy-start = (bf16[64,4,128]{2,1,0:T(4,128)(2,1)S(1)}, bf16[64,4,128]{2,1,0:T(4,128)(2,1)}, u32[]{:S(2)}) copy-start(bf16[64,4,128]{2,1,0:T(4,128)(2,1)} %param.12) | copy-start | bytes 196612
  7.2 32.3 %all-gather.2.cloned.1.call-start = ((), (), s32[]{:S(2)}) async-start(), calls=%async_computation | async-start | bytes 1310720 | tf_op jit(solution)/shard_map/all_gather | solution.py:38
  7.9 8.1 %collective-permute-start = (bf16[16,8192]{1,0:T(8,128)(2,1)}, bf16[16,8192]{1,0:T(8,128)(2,1)S(1)}, u32[]{:S(2)}, u32[]{:S(2)}) collective-permute-start(bf16[16,8192]{1,0:T(8,128)(2,1)} %bitcast.59), channel_id=1, source_target_pairs={{0,4},{4,8},{8,12},{12,16},{16,20},{20,24},{24,28},{28,0},{1,5},{5... | collective-permute-start | bytes 786440 | tf_op jit(solution)/shard_map/ppermute | solution.py:11
  10.6 8.7 %collective-permute-start.2 = (bf16[16,8192]{1,0:T(8,128)(2,1)}, bf16[16,8192]{1,0:T(8,128)(2,1)S(1)}, u32[]{:S(2)}, u32[]{:S(2)}) collective-permute-start(bf16[16,8192]{1,0:T(8,128)(2,1)} %bitcast.60), channel_id=1, source_target_pairs={{0,28},{4,0},{8,4},{12,8},{16,12},{20,16},{24,20},{28,24},{1,29},{... | collective-permute-start | bytes 786440 | tf_op jit(solution)/shard_map/ppermute | solution.py:11
  16.0 6.5 %collective-permute-start.1 = (bf16[16,8192]{1,0:T(8,128)(2,1)S(1)}, bf16[16,8192]{1,0:T(8,128)(2,1)S(1)}, u32[]{:S(2)}, u32[]{:S(2)}) collective-permute-start(bf16[16,8192]{1,0:T(8,128)(2,1)S(1)} %collective-permute-done), channel_id=1, source_target_pairs={{0,4},{4,8},{8,12},{12,16},{16,20},{20,24},{24,28},{28,0},{1,5},{5... | collective-permute-start | bytes 786440 | tf_op jit(solution)/shard_map/ppermute | solution.py:11
  19.3 22.1 %collective-permute-start.3 = (bf16[16,8192]{1,0:T(8,128)(2,1)S(1)}, bf16[16,8192]{1,0:T(8,128)(2,1)S(1)}, u32[]{:S(2)}, u32[]{:S(2)}) collective-permute-start(bf16[16,8192]{1,0:T(8,128)(2,1)S(1)} %collective-permute-done.2), channel_id=1, source_target_pairs={{0,28},{4,0},{8,4},{12,8},{16,12},{20,16},{24,20},{28,24},{1,29},{... | collective-permute-start | bytes 786440 | tf_op jit(solution)/shard_map/ppermute | solution.py:11
  39.5 23.4 %collective-permute-start.4 = (bf16[4,16,8192]{2,1,0:T(8,128)(2,1)}, bf16[4,16,8192]{2,1,0:T(8,128)(2,1)}, u32[]{:S(2)}, u32[]{:S(2)}) collective-permute-start(bf16[4,16,8192]{2,1,0:T(8,128)(2,1)} %all-gather.2.cloned.1.call-done), channel_id=1, source_target_pairs={{0,4},{4,8},{8,12},{12,16},{16,20},{20,24},{24,28},{28,0},{1,5},{5... | collective-permute-start | bytes 3145736 | tf_op jit(solution)/shard_map/ppermute | solution.py:11
  41.4 24.9 %collective-permute-start.5 = (bf16[4,16,8192]{2,1,0:T(8,128)(2,1)}, bf16[4,16,8192]{2,1,0:T(8,128)(2,1)}, u32[]{:S(2)}, u32[]{:S(2)}) collective-permute-start(bf16[4,16,8192]{2,1,0:T(8,128)(2,1)} %all-gather.2.cloned.1.call-done), channel_id=1, source_target_pairs={{0,28},{4,0},{8,4},{12,8},{16,12},{20,16},{24,20},{28,24},{1,29},{... | collective-permute-start | bytes 3145736 | tf_op jit(solution)/shard_map/ppermute | solution.py:11
  51.6 1.1 %copy-start.2 = (f32[1,16,8192]{2,1,0:T(8,128)S(1)}, f32[1,16,8192]{2,1,0:T(8,128)}, u32[]{:S(2)}) copy-start(f32[1,16,8192]{2,1,0:T(8,128)} %param.8) | copy-start | bytes 1572868
  52.6 13.7 %copy-start.1 = (bf16[4,16,8192]{2,1,0:T(8,128)(2,1)S(1)}, bf16[4,16,8192]{2,1,0:T(8,128)(2,1)}, u32[]{:S(2)}) copy-start(bf16[4,16,8192]{2,1,0:T(8,128)(2,1)} %all-gather.2.cloned.1.call-done) | copy-start | bytes 3145732
  68.1 3.9 %copy-start.3 = (f32[16,64]{1,0:T(8,128)S(1)}, f32[16,64]{1,0:T(8,128)}, u32[]{:S(2)}) copy-start(f32[16,64]{1,0:T(8,128)} %param.13) | copy-start | bytes 12292
Sparse Core Ops, SparseCore 0:
  9.6 29.8 all-gather.1
where the time goes:
time: 79.8 us; the launch traced here: 79.5 us
  waiting for transfers between devices  36.8 us (46%)
  between operations  14.2 us (18%)
  matrix products  9.71 us (12%)
  local copies, waits for them, and re-layouts  7.17 us (9%)
  starting transfers between devices  7.01 us (9%)
  other arithmetic  4.68 us (6%)
    ppermute x6, waiting for transfers between devices, from_behind(): lax.ppermute(array, axis, [(i, (i + by) % peers) for i in range(peers)])  19.5 us
    all_gather x1, waiting for transfers between devices, body(): slab_stack = lax.all_gather(currents, 'grp', axis=0, tiled=True)  16.6 us
    dot_general x1, matrix products, body(): jnp.einsum('bkpq,cbkq->cbp', green[0], picked, preferred_element_type=jnp...  8.07 us
    ppermute x6, starting transfers between devices, from_behind(): lax.ppermute(array, axis, [(i, (i + by) % peers) for i in range(peers)])  6.98 us
    gather x1, local copies, waits for them, and re-layouts, body(): chosen = near_blocks[slab_index, :, position, :]  2.19 us
    unnamed x13, local copies, waits for them, and re-layouts  2.17 us
    gather x1, local copies, waits for them, and re-layouts, body(): picked = window_blocks[:, source, :]  2.02 us
    reshape x1, other arithmetic, body(): near_blocks = near.reshape(n_slabs, n_cols, 3 * blocks, cells)  1.81 us
  transfers between devices with their start and end apart: 7, of which 5 were waited for; matrix products, arithmetic and copies ran while one was open for 18% of the time, Pallas kernels for 0%

commit v1 on v0

v1 whole, which is shorter than its diff:
```python
import functools

import jax
import jax.numpy as jnp
from jax import lax
from jax.experimental import pallas as pl
from jax.experimental.pallas import tpu as pltpu
from jax.sharding import PartitionSpec as P

REACH = 2
CHUNKS = 8
MESH = pl.DeviceIdType.MESH


def kernel(
    n_blk, n_grp, cur, green, source, near_any, cells_vm, sgreen, anom, sta,
    win, gbuf, sgf, masked, near_v, near_s, parts, ret,
    gsem, cell_sem, wsend, wrecv, ssend, srecv, csend, crecv, psend, precv,
):
    here = lax.axis_index("blk")
    grp = lax.axis_index("grp")
    blocks, knz, cells = green.shape[0], green.shape[1], green.shape[2]
    n_cols = cur.shape[0]
    n_sta, near = cells_vm.shape
    slab_blocks = blocks * n_blk
    step = blocks // CHUNKS

    def green_copy(i):
        part = pl.ds(i * step, step)
        return pltpu.make_async_copy(green.at[part], gbuf.at[part], gsem.at[i])

    def slot(i):
        return win.at[pl.ds(i * blocks, blocks)]

    own_near = pltpu.make_async_copy(near_any, near_s.at[grp], cell_sem.at[0])
    own_near.start()

    odd = here % 2
    sib = here + 1 - 2 * odd
    up2, down2 = (here + 2) % n_blk, (here + n_blk - 2) % n_blk
    barrier = pltpu.get_barrier_semaphore()
    for peer in (sib, up2, down2):
        pl.semaphore_signal(barrier, inc=1, device_id=(peer, grp), device_id_type=MESH)
    for d in range(1, n_grp):
        pl.semaphore_signal(barrier, inc=1, device_id=(here, (grp + d) % n_grp), device_id_type=MESH)
    for b in range(blocks):
        win[REACH * blocks + b] = cur[:, b * cells : (b + 1) * cells]
    mine = slot(REACH)
    pl.semaphore_wait(barrier, 3 + n_grp - 1)

    def to_blk(src, dst, peer, i):
        return pltpu.make_async_remote_copy(
            src_ref=src, dst_ref=dst, send_sem=wsend.at[i], recv_sem=wrecv.at[i],
            device_id=(peer, grp), device_id_type=MESH,
        )

    c_up = to_blk(mine, slot(0), up2, 0)
    c_down = to_blk(mine, slot(2 * REACH), down2, 1)
    c_sib = to_blk(mine, slot(1 + 2 * odd), sib, 2)
    c_up.start()
    c_down.start()
    c_sib.start()

    def to_grp(src, dst, d, send, recv):
        return pltpu.make_async_remote_copy(
            src_ref=src, dst_ref=dst, send_sem=send.at[d], recv_sem=recv.at[d],
            device_id=(here, (grp + d) % n_grp), device_id_type=MESH,
        )

    c_cells = [None] + [to_grp(near_any, near_v.at[grp], d, csend, crecv) for d in range(1, n_grp)]
    for d in range(1, n_grp):
        c_cells[d].start()

    sgf[...] = sgreen[...].astype(jnp.float32)
    c_rows = [None]
    for d in list(range(1, n_grp)) + [0]:
        peer = (grp + d) % n_grp
        first = peer * slab_blocks
        for k in range(near):
            at = jnp.broadcast_to(cells_vm[:, k : k + 1], (n_sta, cells))
            rows = sgf[pl.ds(k, n_sta, stride=near), :]
            rows = jnp.where((at >= first) & (at < first + slab_blocks), rows, 0.0)
            masked[d, :, k * cells : (k + 1) * cells] = rows.astype(jnp.bfloat16)
        if d > 0:
            c_rows.append(to_grp(masked.at[d], masked.at[n_grp + d], d, ssend, srecv))
            c_rows[d].start()

    for i in range(CHUNKS):
        green_copy(i).start()

    for d in range(1, n_grp):
        c_cells[d].wait_recv()
    c_own = [None]
    for d in range(1, n_grp):
        src = (grp + n_grp - d) % n_grp
        c_own.append(pltpu.make_async_copy(near_v.at[src], near_s.at[src], cell_sem.at[d]))
        c_own[d].start()

    c_up.wait_recv()
    c_down.wait_recv()
    c_fwd = to_blk(slot(2 * REACH * (1 - odd)), slot(3 - 2 * odd), sib, 3)
    c_fwd.start()
    own_near.wait()
    for d in range(1, n_grp):
        c_own[d].wait()
        c_rows[d].wait_recv()
    c_sib.wait_recv()
    c_fwd.wait_recv()

    group = 8
    c_parts = [None]
    for d in list(range(1, n_grp)) + [0]:
        src = (grp + n_grp - d) % n_grp
        rhs_at = n_grp + d if d > 0 else 0

        def stations(t, acc, src=src, rhs_at=rhs_at):
            rows = []
            for s in range(group):
                row = []
                for k in range(near):
                    row.append(win[near_s[src, t * group + s, k]])
                rows.append(jnp.concatenate(row, axis=1))
            lhs = jnp.concatenate(rows, axis=0)
            full = lax.dot_general(
                lhs, masked[rhs_at], (((1,), (1,)), ((), ())), preferred_element_type=jnp.float32
            )
            lane = lax.broadcasted_iota(jnp.int32, acc.shape, 1)
            for s in range(group):
                part = full[s * n_cols : (s + 1) * n_cols, :]
                acc = acc + jnp.where(lane == t * group + s, part, 0.0)
            return acc

        parts[d] = lax.fori_loop(0, n_sta // group, stations, jnp.zeros(parts.shape[1:], jnp.float32))
        if d > 0:
            copy = pltpu.make_async_remote_copy(
                src_ref=parts.at[d], dst_ref=ret.at[d], send_sem=psend.at[d], recv_sem=precv.at[d],
                device_id=(here, src), device_id_type=MESH,
            )
            copy.start()
            c_parts.append(copy)

    for i in range(CHUNKS):
        green_copy(i).wait()

        def row(t, carry, i=i):
            b = i * step + t
            lhs = jnp.concatenate([win[source[b, k]] for k in range(knz)], axis=1)
            rhs = jnp.concatenate([gbuf[b, k] for k in range(knz)], axis=1)
            anom[:, pl.ds(pl.multiple_of(b * cells, 128), cells)] = lax.dot_general(
                lhs, rhs, (((1,), (1,)), ((), ())), preferred_element_type=jnp.float32
            )
            return carry

        lax.fori_loop(0, step, row, 0, unroll=4)

    total = parts[0]
    for d in range(1, n_grp):
        c_parts[d].wait_recv()
        total = total + ret[d]
    sta[...] = total
    for copy in (c_up, c_down, c_sib, c_fwd):
        copy.wait_send()
    for d in range(1, n_grp):
        c_cells[d].wait_send()
        c_rows[d].wait_send()
        c_parts[d].wait_send()


def body(n_blk, n_grp, currents, background, green, offsets, station_cells, station_green, station_background):
    _, n_cols, span = currents.shape
    _, blocks, knz, cells, _ = green.shape
    n_sta, near = station_cells.shape
    here = lax.axis_index("blk")
    slab_blocks = blocks * n_blk
    source = jnp.arange(blocks, dtype=jnp.int32)[:, None] + offsets[0] + REACH * blocks
    position = (station_cells % slab_blocks - (here - 1) * blocks) % slab_blocks + (REACH - 1) * blocks
    any_spec = pl.BlockSpec(memory_space=pl.ANY)
    vmem = pl.BlockSpec(memory_space=pltpu.VMEM)
    dma = pltpu.SemaphoreType.DMA
    anomalous, extra = pl.pallas_call(
        functools.partial(kernel, n_blk, n_grp),
        out_shape=(
            jax.ShapeDtypeStruct((n_cols, span), jnp.float32),
            jax.ShapeDtypeStruct((n_cols, n_sta), jnp.float32),
        ),
        in_specs=[
            vmem, any_spec, pl.BlockSpec(memory_space=pltpu.SMEM), any_spec, vmem, vmem,
        ],
        out_specs=(vmem, vmem),
        scratch_shapes=[
            pltpu.VMEM(((2 * REACH + 1) * blocks, n_cols, cells), jnp.bfloat16),
            pltpu.VMEM((blocks, knz, cells, cells), jnp.bfloat16),
            pltpu.VMEM((n_sta * near, cells), jnp.float32),
            pltpu.VMEM((2 * n_grp, n_sta, near * cells), jnp.bfloat16),
            pltpu.VMEM((n_grp, n_sta, near), jnp.int32),
            pltpu.SMEM((n_grp, n_sta, near), jnp.int32),
            pltpu.VMEM((n_grp, n_cols, n_sta), jnp.float32),
            pltpu.VMEM((n_grp, n_cols, n_sta), jnp.float32),
            dma((CHUNKS,)), dma((n_grp,)), dma((4,)), dma((4,)),
            dma((n_grp,)), dma((n_grp,)), dma((n_grp,)), dma((n_grp,)), dma((n_grp,)), dma((n_grp,)),
        ],
        compiler_params=pltpu.CompilerParams(
            collective_id=0, has_side_effects=True, vmem_limit_bytes=56 * 1024 * 1024
        ),
    )(
        currents[0], green[0], source, position, station_cells,
        station_green.reshape(n_sta * near, cells),
    )
    return background + anomalous[None], station_background + extra


def solution(mesh):
    return jax.shard_map(
        functools.partial(body, mesh.shape["blk"], mesh.shape["grp"]),
        mesh=mesh,
        in_specs=(
            P("grp", None, "blk"),
            P("grp", None, "blk"),
            P("grp", "blk", None, None, None),
            P("grp", "blk", None),
            P(("blk", "grp"), None),
            P(("blk", "grp"), None, None),
            P(None, ("blk", "grp")),
        ),
        out_specs=(P("grp", None, "blk"), P(None, ("blk", "grp"))),
        check_vma=False,
    )
```

time: 79.8 us -> 41.6 us (0.52)
  waiting for transfers between devices: 36.8 us -> 0 us
  Pallas kernels: 0 us -> 33.7 us
  between operations: 14.2 us -> 0.67 us
  matrix products: 9.71 us -> 0 us
  starting transfers between devices: 7.01 us -> 0 us
  local copies, waits for them, and re-layouts: 7.17 us -> 1.67 us
    pallas_call x0 -> x1, Pallas kernels: none -> 33.7 us  [body(): pl.pallas_call(functools.partial(kernel, n_blk, n_grp), out_shape=(jax.Sh...]
    ppermute x6 -> x0, waiting for transfers between devices: 19.5 us -> none  [from_behind(): lax.ppermute(array, axis, [(i, (i + by) % peers) for i in range(peers)])]
    all_gather x1 -> x0, waiting for transfers between devices: 16.6 us -> none  [body(): slab_stack = lax.all_gather(currents, 'grp', axis=0, tiled=True)]
    dot_general x2 -> x0, matrix products: 9.71 us -> none  [the longest x1 8.07 us: body(): jnp.einsum('bkpq,cbkq->cbp', green[0], picked, preferred_element_type=jnp...]
    ppermute x6 -> x0, starting transfers between devices: 6.98 us -> none  [from_behind(): lax.ppermute(array, axis, [(i, (i + by) % peers) for i in range(peers)])]
    gather x2 -> x0, local copies, waits for them, and re-layouts: 4.21 us -> none  [the longest x1 2.19 us: body(): chosen = near_blocks[slab_index, :, position, :]]
    add x2 -> x4, other arithmetic: 1.47 us -> 4.45 us  [the longest x2 3.19 us: body(): return (background + anomalous[None], station_background + extra)]
    reshape x1 -> x0, other arithmetic: 1.81 us -> none  [body(): near_blocks = near.reshape(n_slabs, n_cols, 3 * blocks, cells)]
  transfers between devices with their start and end apart: 7 -> 0, of which waited for: 5 -> 0; matrix products, arithmetic and copies ran while one was open for 18% -> 0% of each run, Pallas kernels for 0% -> 0%
where the time goes in v1:
time: 41.6 us; the launch traced here: 41.3 us
  Pallas kernels  33.7 us (81%)
  other arithmetic  5.19 us (12%)
  local copies, waits for them, and re-layouts  1.67 us (4%)
  between operations  0.67 us (2%)
    pallas_call x1, Pallas kernels, body(): pl.pallas_call(functools.partial(kernel, n_blk, n_grp), out_shape=(jax.Sh...  33.7 us
    add x2, other arithmetic, body(): return (background + anomalous[None], station_background + extra)  3.19 us
    unnamed x8, local copies, waits for them, and re-layouts  1.55 us

profile of v1, /device:TPU:1, one launch (start us, length us, event | category | flops | bytes accessed | tf_op | source)
XLA Modules:
  0.0 41.3 jit_solution(2731789462844824839)
XLA Ops:
  0.6 0.0 copy-start.2
  0.6 0.0 copy-start
  0.7 0.7 %broadcast_compare_fusion = pred[64,4]{0,1:T(4,128)(4,1)S(1)} fusion(s32[64,4]{0,1:T(4,128)} %param.11), kind=kLoop, calls=%fused_computation.13 | loop fusion | flops 256 | bytes 1280 | tf_op jit(solution)/shard_map/jit(remainder)/rem | solution.py:176
  1.4 0.1 copy.14
  1.5 0.8 %copy.11.cells_vm = s32[64,4]{1,0:T(8,128)S(1)} copy(s32[64,4]{0,1:T(4,128)} %param.11) | data formatting | bytes 2048 | tf_op args[4]
  2.3 0.0 copy-start.1
  2.3 0.6 %fusion.3.near_any = s32[64,4]{1,0:T(8,128)} fusion(pred[64,4]{1,0:T(8,128)(4,1)S(1)} %copy.14, s32[64,4]{1,0:T(8,128)S(1)} %copy.11.cells_vm, s32[]{:T(128)S(6)} %mul.3), kind=kLoop, calls=%fused_computation.10 | loop fusion | flops 5888 | bytes 2308 | tf_op jit(solution)/shard_map/add | solution.py:176
  2.9 0.8 %copy.9 = s32[1,64,8]{2,1,0:T(8,128)S(1)} copy(s32[1,64,8]{1,2,0:T(8,128)} %param.10) | data formatting | bytes 4096 | tf_op args[3]
  3.7 0.6 %fusion.4.source = s32[64,8]{1,0:T(8,128)} fusion(s32[1,64,8]{2,1,0:T(8,128)S(1)} %copy.9), kind=kLoop, calls=%fused_computation.12 | loop fusion | flops 1024 | bytes 4096 | tf_op jit(solution)/shard_map/add | solution.py:175
  4.3 0.0 copy-done.1
  4.3 33.7 %shard_map.86 = (f32[16,8192]{1,0:T(8,128)}, f32[16,64]{1,0:T(8,128)}) custom-call(bf16[16,8192]{1,0:T(8,128)(2,1)} %bitcast.10, bf16[64,8,128,128]{3,2,1,0:T(8,128)(2,1)} %bitcast.9, s32[64,8]{1,0:T(8,128)} %fusion.4.source, s32[64,4]{1,0:T(8,128)} %fusion.3.near_any, s32[64,4]{1,0:T(8,128)} %copy-done.1, bf16[256,128]{1,0:T(8,128)(2,1)} %bitcast.11), custom_call_target="tpu_custom_call" | custom-call | tf_op jit(solution)/shard_map/pallas_call | solution.py:180
  38.1 0.0 copy-done
  38.1 1.9 %bitcast_add_fusion = f32[1,16,8192]{2,1,0:T(8,128)} fusion(f32[1,16,8192]{2,1,0:T(8,128)S(1)} %copy-done, f32[16,8192]{1,0:T(8,128)} %get-tuple-element.4), kind=kLoop, calls=%fused_computation | loop fusion | flops 131072 | bytes 1572864 | tf_op jit(solution)/shard_map/add | solution.py:209
  40.0 0.0 copy-done.2
  40.0 1.3 %add.46 = f32[16,64]{1,0:T(8,128)} add(f32[16,64]{1,0:T(8,128)S(1)} %copy-done.2, f32[16,64]{1,0:T(8,128)} %get-tuple-element.5) | non-fusion elementwise | flops 1024 | bytes 12288 | tf_op jit(solution)/shard_map/add | solution.py:209
Async XLA Ops:
  0.6 39.3 %copy-start.2 = (f32[16,64]{1,0:T(8,128)S(1)}, f32[16,64]{1,0:T(8,128)}, u32[]{:S(2)}) copy-start(f32[16,64]{1,0:T(8,128)} %param.13) | copy-start | bytes 12292
  0.6 37.4 %copy-start = (f32[1,16,8192]{2,1,0:T(8,128)S(1)}, f32[1,16,8192]{2,1,0:T(8,128)}, u32[]{:S(2)}) copy-start(f32[1,16,8192]{2,1,0:T(8,128)} %param.8) | copy-start | bytes 1572868
  2.3 2.0 %copy-start.1 = (s32[64,4]{1,0:T(8,128)}, s32[64,4]{1,0:T(8,128)S(1)}, u32[]{:S(2)}) copy-start(s32[64,4]{1,0:T(8,128)S(1)} %copy.11.cells_vm) | copy-start | bytes 3076

commit v2 on v1

v2 whole, which is shorter than its diff:
```python
import functools

import jax
import jax.numpy as jnp
from jax import lax
from jax.experimental import pallas as pl
from jax.experimental.pallas import tpu as pltpu
from jax.sharding import PartitionSpec as P

REACH = 2
CHUNKS = 8
PIECES = 8
LANES = 128
MESH = pl.DeviceIdType.MESH


def kernel(
    n_blk, n_grp, cur_in, green, offs_in, cells_in, rows_in, anom, sta,
    win, gbuf, cur, offs, near_cells, rows, rowf, rhs_st, table, source, near_v, near_s, parts, ret,
    gsem, lsem, tsem, nsem, wsend, wrecv, ssend, srecv, csend, crecv, psend, precv,
):
    here = lax.axis_index("blk")
    grp = lax.axis_index("grp")
    blocks, knz, cells = green.shape[0], green.shape[1], green.shape[2]
    n_cols = cur.shape[0]
    near, n_sta = near_cells.shape
    slab_blocks = blocks * n_blk
    step = blocks // CHUNKS
    nothing = (2 * REACH + 1) * blocks

    odd = here % 2
    sib = here + 1 - 2 * odd
    par = here // 2 % 2
    partner = here + 2 - 4 * par
    far = (here + n_blk + 4 - 8 * par) % n_blk
    far_from = (here + n_blk - 4 + 8 * par) % n_blk
    size = blocks // PIECES
    barrier = pltpu.get_barrier_semaphore()
    for peer in (sib, partner, far_from):
        pl.semaphore_signal(barrier, inc=1, device_id=(peer, grp), device_id_type=MESH)
    for d in range(1, n_grp):
        pl.semaphore_signal(barrier, inc=1, device_id=(here, (grp + d) % n_grp), device_id_type=MESH)

    loads = [
        pltpu.make_async_copy(src, dst, lsem.at[i])
        for i, (src, dst) in enumerate(
            ((cur_in, cur), (cells_in, near_cells), (offs_in, offs), (rows_in, rows.at[0]))
        )
    ]
    for load in loads:
        load.start()

    def green_copy(i):
        part = pl.ds(i * step, step)
        return pltpu.make_async_copy(green.at[part], gbuf.at[part], gsem.at[i])

    def slot(i):
        return win.at[pl.ds(i * blocks, blocks)]

    def chunk_of(i, j):
        return win.at[pl.ds(i * blocks + j * size, size)]

    win[nothing] = jnp.zeros((n_cols, cells), jnp.bfloat16)
    table[...] = jnp.zeros(table.shape, jnp.int32)
    near_v[:n_grp] = jnp.zeros((n_grp,) + near_v.shape[1:], jnp.int32)
    loads[1].wait()
    loads[2].wait()
    table[:knz, :blocks] = offs[...] + lax.broadcasted_iota(jnp.int32, (knz, blocks), 1) + REACH * blocks
    to_source = pltpu.make_async_copy(table, source, tsem)
    to_source.start()
    at = near_cells[...]
    rel = at
    for q in range(1, n_grp):
        rel = jnp.where(at >= q * slab_blocks, at - q * slab_blocks, rel)
    rel = rel - (here - 1) * blocks
    rel = jnp.where(rel < 0, rel + slab_blocks, rel)
    rel = jnp.where(rel >= slab_blocks, rel - slab_blocks, rel) + (REACH - 1) * blocks
    for d in range(n_grp):
        first = (grp + d) % n_grp * slab_blocks
        held = (at >= first) & (at < first + slab_blocks)
        near_v[d, :near, :n_sta] = jnp.where(held, jnp.minimum(rel, nothing), nothing)
    loads[0].wait()
    for b in range(blocks):
        win[REACH * blocks + b] = cur[:, b * cells : (b + 1) * cells]
    mine = slot(REACH)
    pl.semaphore_wait(barrier, 3 + n_grp - 1)

    def to_blk(src, dst, peer, i):
        return pltpu.make_async_remote_copy(
            src_ref=src, dst_ref=dst, send_sem=wsend.at[i], recv_sem=wrecv.at[i],
            device_id=(peer, grp), device_id_type=MESH,
        )

    c_sib = to_blk(mine, slot(1 + 2 * odd), sib, 0)
    c_pair = [to_blk(chunk_of(REACH, j), chunk_of(4 * par, j), partner, 1 + j) for j in range(PIECES)]
    for j in range(PIECES):
        c_pair[j].start()

    def to_grp(src, dst, d, send, recv):
        return pltpu.make_async_remote_copy(
            src_ref=src, dst_ref=dst, send_sem=send.at[d], recv_sem=recv.at[d],
            device_id=(here, (grp + d) % n_grp), device_id_type=MESH,
        )

    c_near, c_rows = [None], [None]
    for d in range(1, n_grp):
        c_near.append(to_grp(near_v.at[d], near_v.at[n_grp + d], d, csend, crecv))
        c_near[d].start()
    for d in range(1, n_grp):
        c_rows.append(to_grp(rows_in, rows.at[d], d, ssend, srecv))
        c_rows[d].start()
    c_sib.start()
    for i in range(CHUNKS):
        green_copy(i).start()
    c_far = []
    for j in range(PIECES):
        c_pair[j].wait_recv()
        c_far.append(to_blk(chunk_of(4 - 4 * par, j), chunk_of(4 * par, j), far, 1 + PIECES + j))
        c_far[j].start()

    to_near = [pltpu.make_async_copy(near_v.at[0], near_s.at[0], nsem.at[0])]
    to_near[0].start()
    for d in range(1, n_grp):
        c_near[d].wait_recv()
        to_near.append(pltpu.make_async_copy(near_v.at[n_grp + d], near_s.at[d], nsem.at[d]))
        to_near[d].start()
    loads[3].wait()
    for d in range(n_grp):
        if d > 0:
            c_rows[d].wait_recv()
        rowf[d] = rows[d].astype(jnp.float32)
        for k in range(near):
            piece = rowf[d, pl.ds(k, n_sta, stride=near), :]
            rhs_st[d, :, k * cells : (k + 1) * cells] = piece.astype(jnp.bfloat16)
    to_source.wait()
    for d in range(n_grp):
        to_near[d].wait()

    c_fwd = []
    for j in range(PIECES):
        c_far[j].wait_recv()
        c_fwd.append(to_blk(chunk_of(4 - 4 * odd, j), chunk_of(3 - 2 * odd, j), sib, 1 + 2 * PIECES + j))
        c_fwd[j].start()
    c_sib.wait_recv()
    for j in range(PIECES):
        c_fwd[j].wait_recv()

    group = 8
    c_parts = [None]
    for d in list(range(1, n_grp)) + [0]:
        src = (grp + n_grp - d) % n_grp

        def stations(t, acc, d=d):
            picks = []
            for s in range(group):
                row = [win[near_s[d, k, t * group + s]] for k in range(near)]
                picks.append(jnp.concatenate(row, axis=1))
            lhs = jnp.concatenate(picks, axis=0)
            full = lax.dot_general(
                lhs, rhs_st[d], (((1,), (1,)), ((), ())), preferred_element_type=jnp.float32
            )
            lane = lax.broadcasted_iota(jnp.int32, acc.shape, 1)
            for s in range(group):
                part = full[s * n_cols : (s + 1) * n_cols, :]
                acc = acc + jnp.where(lane == t * group + s, part, 0.0)
            return acc

        parts[d] = lax.fori_loop(
            0, n_sta // group, stations, jnp.zeros(parts.shape[1:], jnp.float32), unroll=8
        )
        if d > 0:
            copy = pltpu.make_async_remote_copy(
                src_ref=parts.at[d], dst_ref=ret.at[d], send_sem=psend.at[d], recv_sem=precv.at[d],
                device_id=(here, src), device_id_type=MESH,
            )
            copy.start()
            c_parts.append(copy)

    for i in range(CHUNKS):
        green_copy(i).wait()

    def row(b, carry):
        lhs = jnp.concatenate([win[source[k, b]] for k in range(knz)], axis=1)
        rhs = jnp.concatenate([gbuf[b, k] for k in range(knz)], axis=1)
        anom[:, pl.ds(pl.multiple_of(b * cells, 128), cells)] = lax.dot_general(
            lhs, rhs, (((1,), (1,)), ((), ())), preferred_element_type=jnp.float32
        )
        return carry

    lax.fori_loop(0, blocks, row, 0, unroll=8)

    total = parts[0]
    for d in range(1, n_grp):
        c_parts[d].wait_recv()
        total = total + ret[d]
    sta[...] = total
    for copy in [c_sib] + c_pair + c_far + c_fwd:
        copy.wait_send()
    for d in range(1, n_grp):
        c_near[d].wait_send()
        c_rows[d].wait_send()
        c_parts[d].wait_send()


def finish(anom, extra, background, station_background, cell_out, sta_out):
    cell_out[...] = background[...] + anom[...]
    sta_out[...] = station_background[...] + extra[...]


def body(n_blk, n_grp, currents, background, green, offsets, station_cells, station_green, station_background):
    _, n_cols, span = currents.shape
    _, blocks, knz, cells, _ = green.shape
    n_sta, near = station_cells.shape
    hbm = pl.BlockSpec(memory_space=pl.ANY)
    vmem = pl.BlockSpec(memory_space=pltpu.VMEM)
    dma = pltpu.SemaphoreType.DMA
    shapes = (
        jax.ShapeDtypeStruct((n_cols, span), jnp.float32),
        jax.ShapeDtypeStruct((n_cols, n_sta), jnp.float32),
    )
    anomalous, extra = pl.pallas_call(
        functools.partial(kernel, n_blk, n_grp),
        out_shape=shapes,
        in_specs=[hbm] * 5,
        out_specs=(vmem, vmem),
        scratch_shapes=[
            pltpu.VMEM(((2 * REACH + 1) * blocks + 1, n_cols, cells), jnp.bfloat16),
            pltpu.VMEM((blocks, knz, cells, cells), jnp.bfloat16),
            pltpu.VMEM((n_cols, span), jnp.bfloat16),
            pltpu.VMEM((knz, blocks), jnp.int32),
            pltpu.VMEM((near, n_sta), jnp.int32),
            pltpu.VMEM((n_grp, n_sta * near, cells), jnp.bfloat16),
            pltpu.VMEM((n_grp, n_sta * near, cells), jnp.float32),
            pltpu.VMEM((n_grp, n_sta, near * cells), jnp.bfloat16),
            pltpu.VMEM((8, LANES), jnp.int32),
            pltpu.SMEM((8, LANES), jnp.int32),
            pltpu.VMEM((2 * n_grp, 8, LANES), jnp.int32),
            pltpu.SMEM((n_grp, 8, LANES), jnp.int32),
            pltpu.VMEM((n_grp, n_cols, n_sta), jnp.float32),
            pltpu.VMEM((n_grp, n_cols, n_sta), jnp.float32),
            dma((CHUNKS,)), dma((4,)), dma(()), dma((n_grp,)), dma((1 + 3 * PIECES,)), dma((1 + 3 * PIECES,)),
            dma((n_grp,)), dma((n_grp,)), dma((n_grp,)), dma((n_grp,)), dma((n_grp,)), dma((n_grp,)),
        ],
        compiler_params=pltpu.CompilerParams(
            collective_id=0, has_side_effects=True, vmem_limit_bytes=56 * 1024 * 1024
        ),
    )(
        currents[0], green[0], offsets[0].T, station_cells.T,
        station_green.reshape(n_sta * near, cells),
    )
    cell_field, station_field = pl.pallas_call(
        finish, out_shape=shapes, in_specs=[vmem] * 4, out_specs=(vmem, vmem)
    )(anomalous, extra, background[0], station_background)
    return cell_field[None], station_field


def solution(mesh):
    return jax.shard_map(
        functools.partial(body, mesh.shape["blk"], mesh.shape["grp"]),
        mesh=mesh,
        in_specs=(
            P("grp", None, "blk"),
            P("grp", None, "blk"),
            P("grp", "blk", None, None, None),
            P("grp", "blk", None),
            P(("blk", "grp"), None),
            P(("blk", "grp"), None, None),
            P(None, ("blk", "grp")),
        ),
        out_specs=(P("grp", None, "blk"), P(None, ("blk", "grp"))),
        check_vma=False,
    )
```

time: 41.6 us -> 28.4 us (0.68)
  Pallas kernels: 33.7 us -> 27.6 us
  other arithmetic: 5.19 us -> 0 us
  local copies, waits for them, and re-layouts: 1.67 us -> 0 us
    pallas_call x1 -> x2, Pallas kernels: 33.7 us -> 27.6 us  [the longest x1 25.5 us: body(): pl.pallas_call(functools.partial(kernel, n_blk, n_grp), out_shape=shapes,...]
    add x4 -> x0, other arithmetic: 4.45 us -> none  [the longest x2 3.19 us: body(): return (background + anomalous[None], station_background + extra)]
    unnamed x8 -> x0, local copies, waits for them, and re-layouts: 1.55 us -> none
    rem x1 -> x0, other arithmetic: 0.75 us -> none  [body(): station_cells % slab_blocks - (here - 1) * blocks]
where the time goes in v2:
time: 28.4 us; the launch traced here: 28.2 us
  Pallas kernels  27.6 us (97%)
  between operations  0.64 us (2%)
    pallas_call x1, Pallas kernels, body(): pl.pallas_call(functools.partial(kernel, n_blk, n_grp), out_shape=shapes,...  25.5 us
    pallas_call x1, Pallas kernels, body(): pl.pallas_call(finish, out_shape=shapes, in_specs=[vmem] * 4, out_specs=(...  2.07 us

profile of v2, /device:TPU:1, one launch (start us, length us, event | category | flops | bytes accessed | tf_op | source)
XLA Modules:
  0.0 28.2 jit_solution(14259385382842106530)
XLA Ops:
  0.6 25.5 %shard_map.86 = (f32[16,8192]{1,0:T(8,128)}, f32[16,64]{1,0:T(8,128)}) custom-call(bf16[16,8192]{1,0:T(8,128)(2,1)} %bitcast.11, bf16[64,8,128,128]{3,2,1,0:T(8,128)(2,1)} %bitcast.9, s32[8,64]{1,0:T(8,128)} %bitcast.13, s32[4,64]{1,0:T(4,128)} %bitcast.14, bf16[256,128]{1,0:T(8,128)(2,1)} %bitcast.12), custom_call_target="tpu_custom_call" | custom-call | tf_op jit(solution)/shard_map/pallas_call | solution.py:221
  26.1 2.1 %shard_map.87 = (f32[16,8192]{1,0:T(8,128)}, f32[16,64]{1,0:T(8,128)}) custom-call(f32[16,8192]{1,0:T(8,128)} %get-tuple-element.6.anom, f32[16,64]{1,0:T(8,128)} %get-tuple-element.7.extra, f32[16,8192]{1,0:T(8,128)} %bitcast.10, f32[16,64]{1,0:T(8,128)} %station_background.1), custom_call_target="tpu_custom_call" | custom-call | tf_op jit(solution)/shard_map/pallas_call | solution.py:251
